TPU v7x, 256 devices: a whole 4x4x8 slice. The times are simulated.
256 devices in a mesh: seq: 8 (over x_hi, y), row: 32 (over x_lo, z, core).
Axes of the slice: x: 4 (x_hi: 2, x_lo: 2; x = x_hi * 2 + x_lo), y: 4, z: 8, core: 2. Of those that a mesh axis runs over, the one named last changes fastest.
Arguments:
- tokens: bfloat16 [2, 2048, 3072], P(None, ('seq', 'row')), may hold values from -6 to 6
- w_qkv: bfloat16 [6144, 3072], P('row'), may hold values from -0.109375 to 0.109375
- w_rate: bfloat16 [32, 3072], P('row'), may hold values from -0.109375 to 0.109375
- rate_bias: float32 [32], P('row'), may hold values from -3 to 1
- w_out: bfloat16 [2048, 3072], P('row'), may hold values from -0.125 to 0.125
- w_first_init: float32 [32, 64, 256], P('row'), may hold values from -0.75 to 0.75
- b_first_init: float32 [32, 256], P('row'), may hold values from -3 to 3
- w_second_init: float32 [32, 256, 64], P('row'), may hold values from -0.375 to 0.375
- b_second_init: float32 [32, 64], P('row'), may hold values from -3 to 3
- ln_gain: float32 [32, 64], P('row'), may hold values from 0.5 to 1.5
- ln_bias: float32 [32, 64], P('row'), may hold values from -3 to 3
Outputs:
- mixed: bfloat16 [2, 2048, 3072], P(None, ('seq', 'row'))
All inputs are finite; a program needn't handle non-finite values.
Results may differ from a plain program's by a relative error of at most 0.0056.
Values may be sent and summed in bfloat16 or wider, within the bound.
A program may use at most 64 MiB of HBM per device.

v0:
```python
from functools import partial
import jax
import jax.numpy as jnp
from jax import lax
from jax.sharding import PartitionSpec as P

MINI = 64
gelu_coef = 0.7978845608028654
base_rate = 0.01
ln_eps = 1e-06


def passed_along(array, axis, by):
    size = lax.axis_size(axis)
    pairs = [(i, i + by) for i in range(size) if 0 <= i + by < size]
    return lax.ppermute(array, axis, pairs)


def gelu_tanh(entries):
    tanh_arg = gelu_coef * (entries + 0.044715 * entries * entries * entries)
    return 0.5 * entries * (1.0 + jnp.tanh(tanh_arg))


def gelu_slope(entries):
    tanh_arg = gelu_coef * (entries + 0.044715 * entries * entries * entries)
    tangent = jnp.tanh(tanh_arg)
    return 0.5 * (1.0 + tangent) + 0.5 * entries * (1.0 - tangent * tangent) * gelu_coef * (
        1.0 + 3.0 * 0.044715 * entries * entries
    )


def matmul(left, right):
    return jnp.dot(left, right, precision=lax.Precision.HIGHEST, preferred_element_type=jnp.float32)


def normalize(entries):
    centred = entries - jnp.mean(entries, axis=-1, keepdims=True)
    spread = jnp.sqrt(jnp.mean(centred * centred, axis=-1, keepdims=True) + ln_eps)
    return (centred / spread, spread)


def mini_step(inner_state, batch_block, norm_gain, offset):
    w_first, b_first, w_second, b_second = inner_state
    queries, key_rows, value_rows, lr_rows = batch_block
    mini_len = queries.shape[0]
    hidden_pre = matmul(key_rows, w_first) + b_first
    hidden = gelu_tanh(hidden_pre)
    second = matmul(hidden, w_second) + b_second
    target = value_rows - key_rows
    normed, spread = normalize(second)
    grad_out = norm_gain * (norm_gain * normed + offset - target)
    feat_width = second.shape[-1]
    grad_second = (
        feat_width * grad_out
        - jnp.sum(grad_out, axis=-1, keepdims=True)
        - normed * jnp.sum(grad_out * normed, axis=-1, keepdims=True)
    ) / (feat_width * spread)
    grad_first = matmul(grad_second, w_second.T) * gelu_slope(hidden_pre)
    tri_mask = jnp.tril(jnp.ones((mini_len, mini_len), jnp.float32))
    eta_last = lr_rows / mini_len
    eta_table = tri_mask * eta_last[None, :]
    query_keys = matmul(queries, key_rows.T) * eta_table
    bias_first = b_first - matmul(eta_table, grad_first)
    first_bar = matmul(queries, w_first) - matmul(query_keys, grad_first) + bias_first
    hidden_bar = gelu_tanh(first_bar)
    hidden_pairs = matmul(hidden_bar, hidden.T) * eta_table
    bias_second = b_second - matmul(eta_table, grad_second)
    second_bar = matmul(hidden_bar, w_second) - matmul(hidden_pairs, grad_second) + bias_second
    w_first = w_first - matmul((key_rows * eta_last[:, None]).T, grad_first)
    b_first = b_first - matmul(eta_last[None, :], grad_first)[0]
    w_second = w_second - matmul((hidden * eta_last[:, None]).T, grad_second)
    b_second = b_second - matmul(eta_last[None, :], grad_second)[0]
    normed_bar, spread_bar = normalize(second_bar)
    result = queries + norm_gain * normed_bar + offset
    return ((w_first, b_first, w_second, b_second), result)


def run_blocks(inner_state, queries, key_rows, value_rows, lr_rows, norm_gain, offset, mini_len):
    block_count = queries.shape[0] // mini_len
    blocks = (
        queries.reshape(block_count, mini_len, -1),
        key_rows.reshape(block_count, mini_len, -1),
        value_rows.reshape(block_count, mini_len, -1),
        lr_rows.reshape(block_count, mini_len),
    )

    def advance(loop_carry, batch_block):
        return mini_step(loop_carry, batch_block, norm_gain, offset)

    inner_state, results = lax.scan(advance, inner_state, blocks)
    return (inner_state, results.reshape(queries.shape[0], -1))


def pack_state(state):
    videos = state[0].shape[0]
    return jnp.concatenate([part.reshape(videos, -1) for part in state], axis=1)


def unpack_state(flat, like):
    parts = []
    at = 0
    for part in like:
        width = part[0].size
        parts.append(flat[:, at : at + width].reshape(part.shape))
        at += width
    return tuple(parts)


def on_device(
    tokens,
    w_qkv,
    w_rate,
    rate_bias,
    w_out,
    w_first_init,
    b_first_init,
    w_second_init,
    b_second_init,
    ln_gain,
    ln_bias,
):
    videos, tok_part, feat_width = tokens.shape
    row_axes = ("xlo", "z", "core")
    pair_axes = ("xlo", "core")
    row_count = lax.axis_size(row_axes)
    z_count = lax.axis_size("z")
    pair_count = lax.axis_size(pair_axes)
    seg_len = tok_part * row_count
    proj_width = w_qkv.shape[0]
    head_size = proj_width // 3
    stacked = jnp.concatenate([w_qkv, w_rate], axis=0)
    gathered = lax.all_gather(tokens, row_axes, axis=1, tiled=True)
    gathered, w_out = lax.optimization_barrier((gathered, w_out))
    w_out_pair = lax.all_gather(w_out, pair_axes, axis=0, tiled=True)
    combined = jnp.einsum("vkd,cd->vkc", gathered, stacked, preferred_element_type=jnp.float32)
    projected = lax.optimization_barrier(combined[:, :, :proj_width].astype(jnp.bfloat16)).astype(
        jnp.float32
    )
    queries = projected[:, :, :head_size]
    key_rows = projected[:, :, head_size : 2 * head_size]
    value_rows = projected[:, :, 2 * head_size :]
    lr_rows = base_rate * jax.nn.sigmoid(combined[:, :, proj_width] + rate_bias[0])
    initial = (w_first_init[0], b_first_init[0], w_second_init[0], b_second_init[0])
    norm_gain = ln_gain[0]
    offset = ln_bias[0]

    def segment(inner_state, video_q, video_k, video_v, video_lr):
        return run_blocks(inner_state, video_q, video_k, video_v, video_lr, norm_gain, offset, MINI)

    seq_count = lax.axis_size("seq")
    seq_place = lax.axis_index("seq")
    first_device = seq_place == 0

    def spread_videos(entries):
        return jnp.broadcast_to(entries, (videos,) + entries.shape)

    start_states = jax.tree.map(spread_videos, initial)
    incoming = start_states
    for turn_idx in range(seq_count):
        finals, results = jax.vmap(segment)(incoming, queries, key_rows, value_rows, lr_rows)
        if turn_idx + 1 < seq_count:
            with jax.named_scope("state_hop"):
                received = unpack_state(passed_along(pack_state(finals), "seq", 1), finals)
            incoming = jax.tree.map(partial(jnp.where, first_device), start_states, received)
    heads_rows = results.astype(jnp.bfloat16)
    with jax.named_scope("output_mix"):
        by_owner = heads_rows.reshape(videos, 2, z_count, 2, tok_part, head_size)
        by_owner = by_owner.transpose(1, 3, 0, 2, 4, 5).reshape(
            pair_count, videos, z_count, tok_part, head_size
        )
        by_head = lax.all_to_all(by_owner, pair_axes, 0, 0, tiled=True)
        partial_terms = jnp.einsum(
            "gvzic,gcd->zvid",
            by_head,
            w_out_pair.reshape(pair_count, head_size, feat_width),
            preferred_element_type=jnp.float32,
        )
        mixed_out = lax.psum_scatter(
            partial_terms.reshape(z_count, -1), "z", scatter_dimension=0, tiled=True
        )
        mixed_out = lax.optimization_barrier(mixed_out)
    return mixed_out.reshape(videos, tok_part, feat_width).astype(jnp.bfloat16)


def solution(mesh):
    seq_count, row_count = mesh.devices.shape
    fine = jax.sharding.Mesh(
        mesh.devices.reshape(seq_count, 2, row_count // 4, 2), ("seq", "xlo", "z", "core")
    )
    row = ("xlo", "z", "core")
    in_specs = (
        P(None, ("seq",) + row, None),
        P(row, None),
        P(row, None),
        P(row),
        P(row, None),
        P(row, None, None),
        P(row, None),
        P(row, None, None),
        P(row, None),
        P(row, None),
        P(row, None),
    )
    out_specs = P(None, ("seq",) + row, None)
    return jax.shard_map(
        on_device, mesh=fine, in_specs=in_specs, out_specs=out_specs, check_vma=False
    )
```

profile of v0, /device:TPU:4, one launch (start us, length us, event | category | flops | bytes accessed | tf_op | source)
XLA Modules:
  0.0 355.5 jit_solution(17340669928445101169)
XLA Ops:
  6.5 0.7 all-gather.3.cloned.1.call-update
  7.9 70.0 %all-gather.3.cloned.1.call-done = bf16[2,256,3072]{2,1,0:T(8,128)(2,1)} async-done(((bf16[2,8,3072]{2,1,0:T(8,128)(2,1)}), bf16[2,256,3072]{2,1,0:T(8,128)(2,1)}) %all-gather.3.cloned.1.call-update) | async-done | bytes 3145744 | tf_op jit(solution)/shard_map/all_gather | solution.py:132
  78.0 3.4 fusion.200
  82.3 10.8 %while.130 = (s32[]{:T(128)}, f32[2,64,256]{2,1,0:T(8,128)S(1)}, f32[2,256]{1,0:T(2,128)S(1)}, f32[2,256,64]{1,2,0:T(8,128)S(1)}, f32[2,64]{1,0:T(2,128)S(1)}, /...) while((s32[]{:T(128)}, f32[2,64,256]{2,1,0:T(8,128)S(1)}, ...), condition=%wide.region_5.6_spmd, body=%wide.region_0.5_spmd.sunk | while | flops 127755136 | bytes 2386049 | solution.py:90
  93.7 3.4 collective-permute-start
  97.2 10.5 %collective-permute-done = f32[2,33088]{1,0:T(2,128)S(1)} collective-permute-done((f32[2,33088]{1,0:T(2,128)S(1)}, f32[2,33088]{1,0:T(2,128)S(1)}, u32[]{:S(2)}, u32[]{:S(2)}) %collective-permute-start) | collective-permute-done | bytes 264736 | tf_op jit(solution)/shard_map/state_hop/ppermute | solution.py:16
  108.1 10.8 %while.131 = (s32[]{:T(128)}, f32[2,64,256]{2,1,0:T(8,128)S(1)}, f32[2,256]{1,0:T(2,128)S(1)}, f32[2,256,64]{1,2,0:T(8,128)S(1)}, f32[2,64]{1,0:T(2,128)S(1)}, /...) while((s32[]{:T(128)}, f32[2,64,256]{2,1,0:T(8,128)S(1)}, ...), condition=%wide.region_11.12_spmd, body=%wide.region_6.11_spmd.sunk | while | flops 127755136 | bytes 2386049 | solution.py:90
  112.7 0.4 convolution_subtract_fusion.40
  118.1 0.4 convolution_subtract_fusion.40
  119.5 1.9 collective-permute-start.1
  121.4 11.3 %collective-permute-done.1 = f32[2,33088]{1,0:T(2,128)S(1)} collective-permute-done((f32[2,33088]{1,0:T(2,128)S(1)}, f32[2,33088]{1,0:T(2,128)S(1)}, u32[]{:S(2)}, u32[]{:S(2)}) %collective-permute-start.1) | collective-permute-done | bytes 264736 | tf_op jit(solution)/shard_map/state_hop/ppermute | solution.py:16
  133.1 10.8 %while.132 = (s32[]{:T(128)}, f32[2,64,256]{2,1,0:T(8,128)S(1)}, f32[2,256]{1,0:T(2,128)S(1)}, f32[2,256,64]{1,2,0:T(8,128)S(1)}, f32[2,64]{1,0:T(2,128)S(1)}, /...) while((s32[]{:T(128)}, f32[2,64,256]{2,1,0:T(8,128)S(1)}, ...), condition=%wide.region_17.18_spmd, body=%wide.region_12.17_spmd.sunk | while | flops 127755136 | bytes 2386049 | solution.py:90
  137.7 0.4 convolution_subtract_fusion.42
  143.1 0.4 convolution_subtract_fusion.42
  144.4 1.9 collective-permute-start.2
  146.4 10.4 %collective-permute-done.2 = f32[2,33088]{1,0:T(2,128)S(1)} collective-permute-done((f32[2,33088]{1,0:T(2,128)S(1)}, f32[2,33088]{1,0:T(2,128)S(1)}, u32[]{:S(2)}, u32[]{:S(2)}) %collective-permute-start.2) | collective-permute-done | bytes 264736 | tf_op jit(solution)/shard_map/state_hop/ppermute | solution.py:16
  157.1 10.8 %while.133 = (s32[]{:T(128)}, f32[2,64,256]{2,1,0:T(8,128)S(1)}, f32[2,256]{1,0:T(2,128)S(1)}, f32[2,256,64]{1,2,0:T(8,128)S(1)}, f32[2,64]{1,0:T(2,128)S(1)}, /...) while((s32[]{:T(128)}, f32[2,64,256]{2,1,0:T(8,128)S(1)}, ...), condition=%wide.region_23.24_spmd, body=%wide.region_18.23_spmd.sunk | while | flops 127755136 | bytes 2386049 | solution.py:90
  161.7 0.4 convolution_subtract_fusion.44
  167.2 0.4 convolution_subtract_fusion.44
  168.5 2.1 collective-permute-start.3
  170.6 9.8 %collective-permute-done.3 = f32[2,33088]{1,0:T(2,128)S(1)} collective-permute-done((f32[2,33088]{1,0:T(2,128)S(1)}, f32[2,33088]{1,0:T(2,128)S(1)}, u32[]{:S(2)}, u32[]{:S(2)}) %collective-permute-start.3) | collective-permute-done | bytes 264736 | tf_op jit(solution)/shard_map/state_hop/ppermute | solution.py:16
  180.8 10.8 %while.134 = (s32[]{:T(128)}, f32[2,64,256]{2,1,0:T(8,128)S(1)}, f32[2,256]{1,0:T(2,128)S(1)}, f32[2,256,64]{1,2,0:T(8,128)S(1)}, f32[2,64]{1,0:T(2,128)S(1)}, /...) while((s32[]{:T(128)}, f32[2,64,256]{2,1,0:T(8,128)S(1)}, ...), condition=%wide.region_29.30_spmd, body=%wide.region_24.29_spmd.sunk | while | flops 127755136 | bytes 2386049 | solution.py:90
  185.4 0.4 convolution_subtract_fusion.46
  190.8 0.4 convolution_subtract_fusion.46
  192.2 1.9 collective-permute-start.4
  194.1 10.0 %collective-permute-done.4 = f32[2,33088]{1,0:T(2,128)S(1)} collective-permute-done((f32[2,33088]{1,0:T(2,128)S(1)}, f32[2,33088]{1,0:T(2,128)S(1)}, u32[]{:S(2)}, u32[]{:S(2)}) %collective-permute-start.4) | collective-permute-done | bytes 264736 | tf_op jit(solution)/shard_map/state_hop/ppermute | solution.py:16
  204.5 10.8 %while.135 = (s32[]{:T(128)}, f32[2,64,256]{2,1,0:T(8,128)S(1)}, f32[2,256]{1,0:T(2,128)S(1)}, f32[2,256,64]{1,2,0:T(8,128)S(1)}, f32[2,64]{1,0:T(2,128)S(1)}, /...) while((s32[]{:T(128)}, f32[2,64,256]{2,1,0:T(8,128)S(1)}, ...), condition=%wide.region_35.36_spmd, body=%wide.region_30.35_spmd.sunk | while | flops 127755136 | bytes 2386049 | solution.py:90
  209.1 0.4 convolution_subtract_fusion.48
  214.5 0.4 convolution_subtract_fusion.48
  215.8 1.9 collective-permute-start.5
  217.8 10.0 %collective-permute-done.5 = f32[2,33088]{1,0:T(2,128)S(1)} collective-permute-done((f32[2,33088]{1,0:T(2,128)S(1)}, f32[2,33088]{1,0:T(2,128)S(1)}, u32[]{:S(2)}, u32[]{:S(2)}) %collective-permute-start.5) | collective-permute-done | bytes 264736 | tf_op jit(solution)/shard_map/state_hop/ppermute | solution.py:16
  228.2 10.8 %while.136 = (s32[]{:T(128)}, f32[2,64,256]{2,1,0:T(8,128)S(1)}, f32[2,256]{1,0:T(2,128)S(1)}, f32[2,256,64]{1,2,0:T(8,128)S(1)}, f32[2,64]{1,0:T(2,128)S(1)}, /...) while((s32[]{:T(128)}, f32[2,64,256]{2,1,0:T(8,128)S(1)}, ...), condition=%wide.region_41.42_spmd, body=%wide.region_36.41_spmd.sunk | while | flops 127755136 | bytes 2386049 | solution.py:90
  232.8 0.4 convolution_subtract_fusion.50
  238.2 0.4 convolution_subtract_fusion.50
  239.5 1.9 collective-permute-start.6
  241.8 9.6 %collective-permute-done.6 = f32[2,33088]{1,0:T(2,128)S(1)} collective-permute-done((f32[2,33088]{1,0:T(2,128)S(1)}, f32[2,33088]{1,0:T(2,128)S(1)}, u32[]{:S(2)}, u32[]{:S(2)}) %collective-permute-start.6) | collective-permute-done | bytes 264736 | tf_op jit(solution)/shard_map/state_hop/ppermute | solution.py:16
  251.9 20.8 %while.137 = (s32[]{:T(128)}, f32[2,64,256]{2,1,0:T(8,128)S(1)}, f32[2,256]{1,0:T(2,128)S(1)}, f32[2,256,64]{1,2,0:T(8,128)S(1)}, f32[2,64]{1,0:T(2,128)S(1)}, /...) while((s32[]{:T(128)}, f32[2,64,256]{2,1,0:T(8,128)S(1)}, ...), condition=%wide.region_49.50_spmd, body=%wide.region_42.49_spmd.sunk | while | flops 273236992 | bytes 4856473 | solution.py:90
  261.5 0.4 convolution_subtract_fusion.52
  272.7 0.8 reshape.533
  273.5 3.5 all-to-all-start
  277.0 0.6 dynamic-slice
  277.6 3.2 all-to-all-done
  281.0 1.8 convolution_bitcast_fusion
  283.0 0.9 copy.288
  283.9 62.7 %all-reduce.2 = bf16[8,49152]{1,0:T(8,128)(2,1)S(1)} all-reduce(f32[8,49152]{1,0:T(8,128)S(1)} %bitcast.719), channel_id=2, replica_groups=mesh['seq'=8,'xlo'=2,'z'=8,'core'=2] {'z'}, use_global_device_ids=true, to_apply=%region_50.51.clone | all-reduce | flops 393216 | bytes 2359296
  346.6 0.8 constant_dynamic-slice_fusion.1
  347.5 0.6 convert_reduce_fusion
  348.0 0.7 convert_element_type.25
  (666 shorter events, 96.4 us)
Async XLA Ops:
  6.5 71.4 %all-gather.3.cloned.1.call-start = ((), (), s32[]{:S(2)}) async-start(), calls=%async_computation.1 | async-start | bytes 3244032 | tf_op jit(solution)/shard_map/all_gather | solution.py:132
  7.3 273.8 %all-gather.5.cloned.1.call-start = ((), (), s32[]{:S(2)}) async-start(), calls=%async_computation.2 | async-start | bytes 1966080 | tf_op jit(solution)/shard_map/all_gather | solution.py:134
  81.4 0.9 copy-start
  81.4 0.9 copy-start.4
  81.4 0.9 copy-start.5
  81.4 0.9 copy-start.3
  81.4 0.9 copy-start.1
  81.4 0.9 copy-start.2
  93.7 14.0 %collective-permute-start = (f32[2,33088]{1,0:T(2,128)S(1)}, f32[2,33088]{1,0:T(2,128)S(1)}, u32[]{:S(2)}, u32[]{:S(2)}) collective-permute-start(f32[2,33088]{1,0:T(2,128)S(1)} %pad_maximum_fusion), channel_id=1, source_target_pairs={{0,32},{32,64},{64,96},{96,128},{128,160},{160,192},{192,224},{1,3... | collective-permute-start | bytes 794120 | tf_op jit(solution)/shard_map/state_hop/ppermute | solution.py:16
  119.5 13.2 %collective-permute-start.1 = (f32[2,33088]{1,0:T(2,128)S(1)}, f32[2,33088]{1,0:T(2,128)S(1)}, u32[]{:S(2)}, u32[]{:S(2)}) collective-permute-start(f32[2,33088]{1,0:T(2,128)S(1)} %pad_maximum_fusion.1), channel_id=1, source_target_pairs={{0,32},{32,64},{64,96},{96,128},{128,160},{160,192},{192,224},{1,3... | collective-permute-start | bytes 794120 | tf_op jit(solution)/shard_map/state_hop/ppermute | solution.py:16
  144.4 12.3 %collective-permute-start.2 = (f32[2,33088]{1,0:T(2,128)S(1)}, f32[2,33088]{1,0:T(2,128)S(1)}, u32[]{:S(2)}, u32[]{:S(2)}) collective-permute-start(f32[2,33088]{1,0:T(2,128)S(1)} %pad_maximum_fusion.2), channel_id=1, source_target_pairs={{0,32},{32,64},{64,96},{96,128},{128,160},{160,192},{192,224},{1,3... | collective-permute-start | bytes 794120 | tf_op jit(solution)/shard_map/state_hop/ppermute | solution.py:16
  168.5 11.9 %collective-permute-start.3 = (f32[2,33088]{1,0:T(2,128)S(1)}, f32[2,33088]{1,0:T(2,128)S(1)}, u32[]{:S(2)}, u32[]{:S(2)}) collective-permute-start(f32[2,33088]{1,0:T(2,128)S(1)} %pad_maximum_fusion.3), channel_id=1, source_target_pairs={{0,32},{32,64},{64,96},{96,128},{128,160},{160,192},{192,224},{1,3... | collective-permute-start | bytes 794120 | tf_op jit(solution)/shard_map/state_hop/ppermute | solution.py:16
  192.2 11.9 %collective-permute-start.4 = (f32[2,33088]{1,0:T(2,128)S(1)}, f32[2,33088]{1,0:T(2,128)S(1)}, u32[]{:S(2)}, u32[]{:S(2)}) collective-permute-start(f32[2,33088]{1,0:T(2,128)S(1)} %pad_maximum_fusion.4), channel_id=1, source_target_pairs={{0,32},{32,64},{64,96},{96,128},{128,160},{160,192},{192,224},{1,3... | collective-permute-start | bytes 794120 | tf_op jit(solution)/shard_map/state_hop/ppermute | solution.py:16
  215.8 11.9 %collective-permute-start.5 = (f32[2,33088]{1,0:T(2,128)S(1)}, f32[2,33088]{1,0:T(2,128)S(1)}, u32[]{:S(2)}, u32[]{:S(2)}) collective-permute-start(f32[2,33088]{1,0:T(2,128)S(1)} %pad_maximum_fusion.5), channel_id=1, source_target_pairs={{0,32},{32,64},{64,96},{96,128},{128,160},{160,192},{192,224},{1,3... | collective-permute-start | bytes 794120 | tf_op jit(solution)/shard_map/state_hop/ppermute | solution.py:16
  239.5 11.9 %collective-permute-start.6 = (f32[2,33088]{1,0:T(2,128)S(1)}, f32[2,33088]{1,0:T(2,128)S(1)}, u32[]{:S(2)}, u32[]{:S(2)}) collective-permute-start(f32[2,33088]{1,0:T(2,128)S(1)} %pad_maximum_fusion.6), channel_id=1, source_target_pairs={{0,32},{32,64},{64,96},{96,128},{128,160},{160,192},{192,224},{1,3... | collective-permute-start | bytes 794120 | tf_op jit(solution)/shard_map/state_hop/ppermute | solution.py:16
  251.9 25.1 %copy-start.6 = (u32[256]{0:T(256)S(1)}, u32[256]{0:T(256)}, u32[]{:S(2)}) copy-start(u32[256]{0:T(256)} %constant.275) | copy-start | bytes 3076
  273.5 7.4 %all-to-all-start = ((bf16[4,2,4096]{2,1,0:T(2,128)(2,1)}), bf16[4,2,4096]{2,1,0:T(2,128)(2,1)S(1)}, u32[]{:S(2)}, u32[]{:S(2)}) async-start(bf16[4,2,4096]{2,1,0:T(2,128)(2,1)} %reshape.533), calls=%async_computation | async-start | bytes 131072 | tf_op jit(solution)/shard_map/output_mix/all_to_all | solution.py:171
Sparse Core Ops, SparseCore 0:
  9.2 68.7 all-gather.2
  241.9 27.2 all-gather.4
where the time goes:
time: 356 us
  waiting for transfers between devices  146 us (41%)
  matrix products  78.5 us (22%)
  blocking collectives  62.7 us (18%)
  other arithmetic  21.7 us (6%)
  starting transfers between devices  18.6 us (5%)
  between operations  14.9 us (4%)
  local copies, waits for them, and re-layouts  10.9 us (3%)
    dot_general x256, matrix products, matmul(): jnp.dot(left, right, precision=lax.Precision.HIGHEST, preferred_element_t...  73.3 us
    ppermute x7, waiting for transfers between devices, passed_along(): return lax.ppermute(array, axis, pairs)  71.6 us
    all_gather x1, waiting for transfers between devices, on_device(): gathered = lax.all_gather(tokens, row_axes, axis=1, tiled=True)  70 us
    unnamed x1, blocking collectives  62.7 us
    ppermute x7, starting transfers between devices, passed_along(): return lax.ppermute(array, axis, pairs)  15.1 us
  transfers between devices with their start and end apart: 10, of which 9 were waited for; matrix products, arithmetic and copies ran while one was open for 6% of the time, Pallas kernels for 0%

commit v1 on v0

--- a/solution.py
+++ b/solution.py
@@ -129,7 +129,9 @@
     proj_width = w_qkv.shape[0]
     head_size = proj_width // 3
     stacked = jnp.concatenate([w_qkv, w_rate], axis=0)
-    gathered = lax.all_gather(tokens, row_axes, axis=1, tiled=True)
+    gathered = jnp.concatenate(
+        lax.all_to_all(jnp.stack([tokens] * lax.axis_size(row_axes)), row_axes, 0, 0), axis=1
+    )
     gathered, w_out = lax.optimization_barrier((gathered, w_out))
     w_out_pair = lax.all_gather(w_out, pair_axes, axis=0, tiled=True)
     combined = jnp.einsum("vkd,cd->vkc", gathered, stacked, preferred_element_type=jnp.float32)

time: 356 us -> 368 us (1.034)
  starting transfers between devices: 18.6 us -> 28.2 us
  local copies, waits for them, and re-layouts: 10.9 us -> 15.1 us
    all_to_all x0 -> x1, waiting for transfers between devices: none -> 72.1 us  [on_device(): lax.all_to_all(jnp.stack([tokens] * lax.axis_size(row_axes)), row_axes, 0...]
    all_gather x1 -> x0, waiting for transfers between devices: 70 us -> none  [on_device(): gathered = lax.all_gather(tokens, row_axes, axis=1, tiled=True)]
    all_to_all x0 -> x1, starting transfers between devices: none -> 9.49 us  [on_device(): lax.all_to_all(jnp.stack([tokens] * lax.axis_size(row_axes)), row_axes, 0...]
where the time goes in v1:
time: 368 us; the launch traced here: 367 us
  waiting for transfers between devices  145 us (39%)
  matrix products  76.3 us (21%)
  blocking collectives  63.4 us (17%)
  starting transfers between devices  28.2 us (8%)
  other arithmetic  21.7 us (6%)
  local copies, waits for them, and re-layouts  15.1 us (4%)
  between operations  14.9 us (4%)
    dot_general x256, matrix products, matmul(): jnp.dot(left, right, precision=lax.Precision.HIGHEST, preferred_element_t...  73.3 us
    all_to_all x1, waiting for transfers between devices, on_device(): lax.all_to_all(jnp.stack([tokens] * lax.axis_size(row_axes)), row_axes, 0...  72.1 us
    ppermute x7, waiting for transfers between devices, passed_along(): return lax.ppermute(array, axis, pairs)  69.5 us
    unnamed x1, blocking collectives  63.4 us
    ppermute x7, starting transfers between devices, passed_along(): return lax.ppermute(array, axis, pairs)  15.4 us
    all_to_all x1, starting transfers between devices, on_device(): lax.all_to_all(jnp.stack([tokens] * lax.axis_size(row_axes)), row_axes, 0...  9.49 us
  transfers between devices with their start and end apart: 10, of which 9 were waited for; matrix products, arithmetic and copies ran while one was open for 6% of the time, Pallas kernels for 0%

profile of v1, /device:TPU:4, one launch (start us, length us, event | category | flops | bytes accessed | tf_op | source)
XLA Modules:
  0.0 367.3 jit_solution(11450182284471782767)
XLA Ops:
  6.5 2.9 stack.2
  9.5 9.5 %all-to-all-start = ((bf16[32,2,8,3072]{3,2,1,0:T(8,128)(2,1)}), bf16[32,2,8,3072]{3,2,1,0:T(8,128)(2,1)S(1)}, u32[]{:S(2)}, u32[]{:S(2)}) async-start(bf16[32,2,8,3072]{3,2,1,0:T(8,128)(2,1)} %stack.2), calls=%async_computation | async-start | bytes 6291456 | tf_op jit(solution)/shard_map/all_to_all | solution.py:133
  19.7 72.1 %all-to-all-done = bf16[32,2,8,3072]{3,2,1,0:T(8,128)(2,1)S(1)} async-done(((bf16[32,2,8,3072]{3,2,1,0:T(8,128)(2,1)}), bf16[32,2,8,3072]{3,2,1,0:T(8,128)(2,1)S(1)}, u32[]{:S(2)}, u32[]{:S(2)}) %all-to-all-start) | async-done | bytes 3145760 | tf_op jit(solution)/shard_map/all_to_all | solution.py:133
  92.0 1.0 copy-done.6
  93.0 1.2 fusion.200
  95.2 10.8 %while.130 = (s32[]{:T(128)}, f32[2,64,256]{2,1,0:T(8,128)S(1)}, f32[2,256]{1,0:T(2,128)S(1)}, f32[2,256,64]{1,2,0:T(8,128)S(1)}, f32[2,64]{1,0:T(2,128)S(1)}, /...) while((s32[]{:T(128)}, f32[2,64,256]{2,1,0:T(8,128)S(1)}, ...), condition=%wide.region_5.6_spmd, body=%wide.region_0.5_spmd.sunk | while | flops 127755136 | bytes 2386049 | solution.py:90
  97.1 0.4 convolution_subtract_fusion.38
  102.5 0.4 convolution_subtract_fusion.38
  106.5 3.5 collective-permute-start
  110.1 9.8 %collective-permute-done = f32[2,33088]{1,0:T(2,128)S(1)} collective-permute-done((f32[2,33088]{1,0:T(2,128)S(1)}, f32[2,33088]{1,0:T(2,128)S(1)}, u32[]{:S(2)}, u32[]{:S(2)}) %collective-permute-start) | collective-permute-done | bytes 264736 | tf_op jit(solution)/shard_map/state_hop/ppermute | solution.py:16
  120.3 10.8 %while.131 = (s32[]{:T(128)}, f32[2,64,256]{2,1,0:T(8,128)S(1)}, f32[2,256]{1,0:T(2,128)S(1)}, f32[2,256,64]{1,2,0:T(8,128)S(1)}, f32[2,64]{1,0:T(2,128)S(1)}, /...) while((s32[]{:T(128)}, f32[2,64,256]{2,1,0:T(8,128)S(1)}, ...), condition=%wide.region_11.12_spmd, body=%wide.region_6.11_spmd.sunk | while | flops 127755136 | bytes 2386049 | solution.py:90
  127.6 0.4 convolution_subtract_fusion.40
  130.3 0.4 convolution_subtract_fusion.40
  131.7 1.9 collective-permute-start.1
  133.6 10.5 %collective-permute-done.1 = f32[2,33088]{1,0:T(2,128)S(1)} collective-permute-done((f32[2,33088]{1,0:T(2,128)S(1)}, f32[2,33088]{1,0:T(2,128)S(1)}, u32[]{:S(2)}, u32[]{:S(2)}) %collective-permute-start.1) | collective-permute-done | bytes 264736 | tf_op jit(solution)/shard_map/state_hop/ppermute | solution.py:16
  144.6 10.8 %while.132 = (s32[]{:T(128)}, f32[2,64,256]{2,1,0:T(8,128)S(1)}, f32[2,256]{1,0:T(2,128)S(1)}, f32[2,256,64]{1,2,0:T(8,128)S(1)}, f32[2,64]{1,0:T(2,128)S(1)}, /...) while((s32[]{:T(128)}, f32[2,64,256]{2,1,0:T(8,128)S(1)}, ...), condition=%wide.region_17.18_spmd, body=%wide.region_12.17_spmd.sunk | while | flops 127755136 | bytes 2386049 | solution.py:90
  149.2 0.4 convolution_subtract_fusion.42
  151.9 0.4 convolution_subtract_fusion.42
  154.6 0.4 convolution_subtract_fusion.42
  155.9 2.1 collective-permute-start.2
  158.0 9.8 %collective-permute-done.2 = f32[2,33088]{1,0:T(2,128)S(1)} collective-permute-done((f32[2,33088]{1,0:T(2,128)S(1)}, f32[2,33088]{1,0:T(2,128)S(1)}, u32[]{:S(2)}, u32[]{:S(2)}) %collective-permute-start.2) | collective-permute-done | bytes 264736 | tf_op jit(solution)/shard_map/state_hop/ppermute | solution.py:16
  168.2 10.8 %while.133 = (s32[]{:T(128)}, f32[2,64,256]{2,1,0:T(8,128)S(1)}, f32[2,256]{1,0:T(2,128)S(1)}, f32[2,256,64]{1,2,0:T(8,128)S(1)}, f32[2,64]{1,0:T(2,128)S(1)}, /...) while((s32[]{:T(128)}, f32[2,64,256]{2,1,0:T(8,128)S(1)}, ...), condition=%wide.region_23.24_spmd, body=%wide.region_18.23_spmd.sunk | while | flops 127755136 | bytes 2386049 | solution.py:90
  172.8 0.4 convolution_subtract_fusion.44
  175.5 0.4 convolution_subtract_fusion.44
  178.2 0.4 convolution_subtract_fusion.44
  179.6 1.9 collective-permute-start.3
  181.5 10.0 %collective-permute-done.3 = f32[2,33088]{1,0:T(2,128)S(1)} collective-permute-done((f32[2,33088]{1,0:T(2,128)S(1)}, f32[2,33088]{1,0:T(2,128)S(1)}, u32[]{:S(2)}, u32[]{:S(2)}) %collective-permute-start.3) | collective-permute-done | bytes 264736 | tf_op jit(solution)/shard_map/state_hop/ppermute | solution.py:16
  191.9 10.8 %while.134 = (s32[]{:T(128)}, f32[2,64,256]{2,1,0:T(8,128)S(1)}, f32[2,256]{1,0:T(2,128)S(1)}, f32[2,256,64]{1,2,0:T(8,128)S(1)}, f32[2,64]{1,0:T(2,128)S(1)}, /...) while((s32[]{:T(128)}, f32[2,64,256]{2,1,0:T(8,128)S(1)}, ...), condition=%wide.region_29.30_spmd, body=%wide.region_24.29_spmd.sunk | while | flops 127755136 | bytes 2386049 | solution.py:90
  196.5 0.4 convolution_subtract_fusion.46
  203.3 1.9 collective-permute-start.4
  205.2 10.0 %collective-permute-done.4 = f32[2,33088]{1,0:T(2,128)S(1)} collective-permute-done((f32[2,33088]{1,0:T(2,128)S(1)}, f32[2,33088]{1,0:T(2,128)S(1)}, u32[]{:S(2)}, u32[]{:S(2)}) %collective-permute-start.4) | collective-permute-done | bytes 264736 | tf_op jit(solution)/shard_map/state_hop/ppermute | solution.py:16
  215.6 10.8 %while.135 = (s32[]{:T(128)}, f32[2,64,256]{2,1,0:T(8,128)S(1)}, f32[2,256]{1,0:T(2,128)S(1)}, f32[2,256,64]{1,2,0:T(8,128)S(1)}, f32[2,64]{1,0:T(2,128)S(1)}, /...) while((s32[]{:T(128)}, f32[2,64,256]{2,1,0:T(8,128)S(1)}, ...), condition=%wide.region_35.36_spmd, body=%wide.region_30.35_spmd.sunk | while | flops 127755136 | bytes 2386049 | solution.py:90
  226.9 1.9 collective-permute-start.5
  228.9 10.0 %collective-permute-done.5 = f32[2,33088]{1,0:T(2,128)S(1)} collective-permute-done((f32[2,33088]{1,0:T(2,128)S(1)}, f32[2,33088]{1,0:T(2,128)S(1)}, u32[]{:S(2)}, u32[]{:S(2)}) %collective-permute-start.5) | collective-permute-done | bytes 264736 | tf_op jit(solution)/shard_map/state_hop/ppermute | solution.py:16
  239.3 10.8 %while.136 = (s32[]{:T(128)}, f32[2,64,256]{2,1,0:T(8,128)S(1)}, f32[2,256]{1,0:T(2,128)S(1)}, f32[2,256,64]{1,2,0:T(8,128)S(1)}, f32[2,64]{1,0:T(2,128)S(1)}, /...) while((s32[]{:T(128)}, f32[2,64,256]{2,1,0:T(8,128)S(1)}, ...), condition=%wide.region_41.42_spmd, body=%wide.region_36.41_spmd.sunk | while | flops 127755136 | bytes 2386049 | solution.py:90
  250.6 2.1 collective-permute-start.6
  253.1 9.4 %collective-permute-done.6 = f32[2,33088]{1,0:T(2,128)S(1)} collective-permute-done((f32[2,33088]{1,0:T(2,128)S(1)}, f32[2,33088]{1,0:T(2,128)S(1)}, u32[]{:S(2)}, u32[]{:S(2)}) %collective-permute-start.6) | collective-permute-done | bytes 264736 | tf_op jit(solution)/shard_map/state_hop/ppermute | solution.py:16
  263.0 20.7 %while.137 = (s32[]{:T(128)}, f32[2,64,256]{2,1,0:T(8,128)S(1)}, f32[2,256]{1,0:T(2,128)S(1)}, f32[2,256,64]{1,2,0:T(8,128)S(1)}, f32[2,64]{1,0:T(2,128)S(1)}, /...) while((s32[]{:T(128)}, f32[2,64,256]{2,1,0:T(8,128)S(1)}, ...), condition=%wide.region_49.50_spmd, body=%wide.region_42.49_spmd.sunk | while | flops 273236992 | bytes 4856473 | solution.py:90
  283.8 0.8 reshape.543
  284.6 3.3 all-to-all-start.1
  287.9 0.6 dynamic-slice
  288.5 3.5 all-to-all-done.1
  292.1 1.8 convolution_bitcast_fusion
  294.1 0.9 copy.289
  295.0 63.4 %all-reduce.2 = bf16[8,49152]{1,0:T(8,128)(2,1)S(1)} all-reduce(f32[8,49152]{1,0:T(8,128)S(1)} %bitcast.724), channel_id=2, replica_groups=mesh['seq'=8,'xlo'=2,'z'=8,'core'=2] {'z'}, use_global_device_ids=true, to_apply=%region_50.51.clone | all-reduce | flops 393216 | bytes 2359296
  358.4 0.8 constant_dynamic-slice_fusion.1
  359.2 0.6 convert_reduce_fusion
  359.7 0.7 convert_element_type.25
  (671 shorter events, 97.4 us)
Async XLA Ops:
  9.5 82.3 %all-to-all-start = ((bf16[32,2,8,3072]{3,2,1,0:T(8,128)(2,1)}), bf16[32,2,8,3072]{3,2,1,0:T(8,128)(2,1)S(1)}, u32[]{:S(2)}, u32[]{:S(2)}) async-start(bf16[32,2,8,3072]{3,2,1,0:T(8,128)(2,1)} %stack.2), calls=%async_computation | async-start | bytes 6291456 | tf_op jit(solution)/shard_map/all_to_all | solution.py:133
  19.0 273.1 %all-gather.2.cloned.1.call-start = ((), (), s32[]{:S(2)}) async-start(), calls=%async_computation.2 | async-start | bytes 1966080 | tf_op jit(solution)/shard_map/all_gather | solution.py:136
  19.7 72.3 %copy-start.7 = (bf16[1,3072]{1,0:T(2,128)(2,1)S(1)}, bf16[1,3072]{1,0:T(2,128)(2,1)}, u32[]{:S(2)}) copy-start(bf16[1,3072]{1,0:T(2,128)(2,1)} %param.29) | copy-start | bytes 18436
  91.8 1.3 copy-start.6
  94.2 0.9 copy-start
  94.2 0.9 copy-start.4
  94.2 0.9 copy-start.5
  94.2 0.9 copy-start.3
  94.3 0.9 copy-start.1
  94.3 0.9 copy-start.2
  106.5 13.4 %collective-permute-start = (f32[2,33088]{1,0:T(2,128)S(1)}, f32[2,33088]{1,0:T(2,128)S(1)}, u32[]{:S(2)}, u32[]{:S(2)}) collective-permute-start(f32[2,33088]{1,0:T(2,128)S(1)} %pad_maximum_fusion), channel_id=1, source_target_pairs={{0,32},{32,64},{64,96},{96,128},{128,160},{160,192},{192,224},{1,3... | collective-permute-start | bytes 794120 | tf_op jit(solution)/shard_map/state_hop/ppermute | solution.py:16
  131.7 12.5 %collective-permute-start.1 = (f32[2,33088]{1,0:T(2,128)S(1)}, f32[2,33088]{1,0:T(2,128)S(1)}, u32[]{:S(2)}, u32[]{:S(2)}) collective-permute-start(f32[2,33088]{1,0:T(2,128)S(1)} %pad_maximum_fusion.1), channel_id=1, source_target_pairs={{0,32},{32,64},{64,96},{96,128},{128,160},{160,192},{192,224},{1,3... | collective-permute-start | bytes 794120 | tf_op jit(solution)/shard_map/state_hop/ppermute | solution.py:16
  155.9 11.9 %collective-permute-start.2 = (f32[2,33088]{1,0:T(2,128)S(1)}, f32[2,33088]{1,0:T(2,128)S(1)}, u32[]{:S(2)}, u32[]{:S(2)}) collective-permute-start(f32[2,33088]{1,0:T(2,128)S(1)} %pad_maximum_fusion.2), channel_id=1, source_target_pairs={{0,32},{32,64},{64,96},{96,128},{128,160},{160,192},{192,224},{1,3... | collective-permute-start | bytes 794120 | tf_op jit(solution)/shard_map/state_hop/ppermute | solution.py:16
  179.6 11.9 %collective-permute-start.3 = (f32[2,33088]{1,0:T(2,128)S(1)}, f32[2,33088]{1,0:T(2,128)S(1)}, u32[]{:S(2)}, u32[]{:S(2)}) collective-permute-start(f32[2,33088]{1,0:T(2,128)S(1)} %pad_maximum_fusion.3), channel_id=1, source_target_pairs={{0,32},{32,64},{64,96},{96,128},{128,160},{160,192},{192,224},{1,3... | collective-permute-start | bytes 794120 | tf_op jit(solution)/shard_map/state_hop/ppermute | solution.py:16
  203.3 11.9 %collective-permute-start.4 = (f32[2,33088]{1,0:T(2,128)S(1)}, f32[2,33088]{1,0:T(2,128)S(1)}, u32[]{:S(2)}, u32[]{:S(2)}) collective-permute-start(f32[2,33088]{1,0:T(2,128)S(1)} %pad_maximum_fusion.4), channel_id=1, source_target_pairs={{0,32},{32,64},{64,96},{96,128},{128,160},{160,192},{192,224},{1,3... | collective-permute-start | bytes 794120 | tf_op jit(solution)/shard_map/state_hop/ppermute | solution.py:16
  226.9 11.9 %collective-permute-start.5 = (f32[2,33088]{1,0:T(2,128)S(1)}, f32[2,33088]{1,0:T(2,128)S(1)}, u32[]{:S(2)}, u32[]{:S(2)}) collective-permute-start(f32[2,33088]{1,0:T(2,128)S(1)} %pad_maximum_fusion.5), channel_id=1, source_target_pairs={{0,32},{32,64},{64,96},{96,128},{128,160},{160,192},{192,224},{1,3... | collective-permute-start | bytes 794120 | tf_op jit(solution)/shard_map/state_hop/ppermute | solution.py:16
  250.6 11.9 %collective-permute-start.6 = (f32[2,33088]{1,0:T(2,128)S(1)}, f32[2,33088]{1,0:T(2,128)S(1)}, u32[]{:S(2)}, u32[]{:S(2)}) collective-permute-start(f32[2,33088]{1,0:T(2,128)S(1)} %pad_maximum_fusion.6), channel_id=1, source_target_pairs={{0,32},{32,64},{64,96},{96,128},{128,160},{160,192},{192,224},{1,3... | collective-permute-start | bytes 794120 | tf_op jit(solution)/shard_map/state_hop/ppermute | solution.py:16
  263.0 24.9 %copy-start.8 = (u32[256]{0:T(256)S(1)}, u32[256]{0:T(256)}, u32[]{:S(2)}) copy-start(u32[256]{0:T(256)} %constant.275) | copy-start | bytes 3076
  284.6 7.4 %all-to-all-start.1 = ((bf16[4,2,4096]{2,1,0:T(2,128)(2,1)}), bf16[4,2,4096]{2,1,0:T(2,128)(2,1)S(1)}, u32[]{:S(2)}, u32[]{:S(2)}) async-start(bf16[4,2,4096]{2,1,0:T(2,128)(2,1)} %reshape.543), calls=%async_computation.1 | async-start | bytes 131072 | tf_op jit(solution)/shard_map/output_mix/all_to_all | solution.py:173
Sparse Core Ops, SparseCore 0:
  253.2 26.6 all-gather.1
